TPU v7x, 32 devices: a whole 2x2x4 slice. The times are simulated.
32 devices in a mesh: groups: 2 (over y), row: 4 (over x, core), col: 4 (over z).
Axes of the slice: x: 2, y: 2, z: 4, core: 2. Of those that a mesh axis runs over, the one named last changes fastest.
Arguments:
- slope_matrix: bfloat16 [1024, 1024], P(('groups', 'row'), 'col'), parts along dimension 0, may hold values from -0.3125 to 0.3125
- prior_matrix: bfloat16 [1024, 1024], P(('groups', 'row'), 'col'), parts along dimension 0, may hold values from -0.3125 to 0.3125
- slope_blocks: int32 [8, 8], P(('groups', 'row'), 'col'), parts along dimension 0, may hold values from 0 to 23, as said below
- prior_blocks: int32 [8, 8], P(('groups', 'row'), 'col'), parts along dimension 0, may hold values from 0 to 23, as said below
- weight_ids: int32 [512], P(('groups', 'row')), parts along dimension 0, may hold values from 0 to 15
- valid_mask: int32 [512], P(('groups', 'row')), parts along dimension 0, may hold values 0 or 1
- noise_weights: float32 [32], P('groups'), parts along dimension 0, may hold values from 0.25 to 4
- prior_weights: bfloat16 [1024], P(('groups', 'row')), parts along dimension 0, may hold values from 0.19921875 to 2
- frames: float32 [6144, 64], P(('groups', 'row', 'col')), parts along dimension 0, may hold values from -6 to 6
Outputs:
- gram_matrix: float32 [6144, 3072], P(('groups', 'row'), 'col'), parts along dimension 0
- applied: float32 [6144, 64], P(('groups', 'row', 'col')), parts along dimension 0
There are 2 independent parts, one for each index of `groups`. A program takes and returns all parts, laid end to end along the dimension named above; each array names one. Nothing has to cross between parts.
Inputs may be any that keep to these rules, and one draw needn't show every extreme that they name: `slope_blocks`: row i names, for each block-column set c (entries c * 2 to c * 2 + 1), 2 distinct actuator blocks of that set, c * 6 to c * 6 + 5, in the order in which their blocks are stored. `prior_blocks`: row i names, for each block-column set c (entries c * 2 to c * 2 + 1), 2 distinct actuator blocks of that set, c * 6 to c * 6 + 5, in the order in which their blocks are stored.
All inputs are finite; a program needn't handle non-finite values. No bound on the sum of `valid_mask` on one device may be relied on, other than what follows from the above.
Results may differ from a plain program's by a relative error of at most 0.007.
Values may be sent and summed in bfloat16 or wider, within the bound.
No kernel may reach another device: no remote copies, remote signals or barrier semaphores. Data moves between devices by JAX's collectives and lax.ppermute only.
A program may use at most 128 MiB of HBM per device.

v0:
```python
import jax
import jax.numpy as jnp
from jax import lax
from jax.sharding import PartitionSpec as P

BS = 128
AB = 6


def from_root(block, axis, owner):
    block = jnp.where(lax.axis_index(axis) == owner, block, jnp.zeros_like(block))
    return lax.psum(block, axis)


def expand_blocks(values, block_ids, set_index):
    block_count = block_ids.shape[0]
    chosen = block_ids.shape[1]
    targets = set_index * AB + jnp.arange(AB, dtype=jnp.int32)
    onehot = (block_ids[:, :, None] == targets[None, None, :]).astype(jnp.bfloat16)
    shaped = values.reshape(block_count, BS, chosen, BS)
    expanded = jnp.einsum("rskb,rka->rsab", shaped, onehot, preferred_element_type=jnp.float32)
    return expanded.astype(jnp.bfloat16).reshape(block_count * BS, AB * BS)


def shards(
    slope_matrix,
    prior_matrix,
    slope_blocks,
    prior_blocks,
    weight_ids,
    valid_mask,
    noise_weights,
    prior_weights,
    frames,
):
    row_index = lax.axis_index("row")
    col_index = lax.axis_index("col")
    classes = jnp.arange(noise_weights.shape[0], dtype=jnp.int32)
    picked = jnp.sum(
        jnp.where(weight_ids[:, None] == classes[None, :], noise_weights[None, :], 0.0), axis=1
    )
    subap_weight = picked * valid_mask.astype(jnp.float32)
    slope_weight = jnp.repeat(subap_weight, 2).astype(jnp.bfloat16)
    local_rows = jnp.concatenate([slope_matrix, prior_matrix], axis=0)
    local_ids = jnp.concatenate([slope_blocks, prior_blocks], axis=0)
    local_weight = jnp.concatenate([slope_weight, prior_weights], axis=0)
    all_rows, all_ids, all_weight = (
        lax.all_gather(local_rows, "row", axis=0, tiled=True),
        lax.all_gather(local_ids, "row", axis=0, tiled=True),
        lax.all_gather(local_weight, "row", axis=0, tiled=True),
    )
    row_scale = all_weight.astype(jnp.float32)[:, None]
    weighted_rows = (all_rows.astype(jnp.float32) * row_scale).astype(jnp.bfloat16)
    weighted_cols = expand_blocks(weighted_rows, all_ids, col_index)
    sent_rows, sent_ids = (
        from_root(all_rows, "col", row_index),
        from_root(all_ids, "col", row_index),
    )
    row_dense = expand_blocks(sent_rows, sent_ids, row_index)
    gram_tile = lax.dot_general(
        row_dense, weighted_cols, (((0,), (0,)), ((), ())), preferred_element_type=jnp.float32
    )
    frames_rows = lax.all_gather(frames, "col", axis=0, tiled=True)
    frames_cols = from_root(frames_rows, "row", col_index)
    partial_image = jnp.dot(
        gram_tile, frames_cols, precision=lax.Precision.HIGHEST, preferred_element_type=jnp.float32
    )
    applied = lax.psum_scatter(partial_image, "col", scatter_dimension=0, tiled=True)
    return (gram_tile, applied)


def solution(mesh):
    in_specs = (
        P(("groups", "row"), "col"),
        P(("groups", "row"), "col"),
        P(("groups", "row"), "col"),
        P(("groups", "row"), "col"),
        P(("groups", "row")),
        P(("groups", "row")),
        P("groups"),
        P(("groups", "row")),
        P(("groups", "row", "col"), None),
    )
    out_specs = (P(("groups", "row"), "col"), P(("groups", "row", "col"), None))
    return jax.shard_map(shards, mesh=mesh, in_specs=in_specs, out_specs=out_specs, check_vma=False)
```

profile of v0, /device:TPU:0, one launch (start us, length us, event | category | flops | bytes accessed | tf_op | source)
XLA Modules:
  0.0 126.3 jit_solution(12584636910592303553)
XLA Ops:
  7.2 0.0 copy-start.2
  7.2 0.0 all-reduce.3.cloned.1.call-start
  7.2 0.9 pad_maximum_fusion
  8.1 8.6 %all_gather.13 = bf16[1024,256]{1,0:T(8,128)(2,1)S(1)} all-gather(bf16[256,256]{1,0:T(8,128)(2,1)S(1)} %pad_maximum_fusion), channel_id=1, replica_groups=mesh['groups'=2,'row'=4,'col'=4] {'row'}, dimensions={0}, use_global_device_ids=true | all-gather | bytes 655360 | tf_op jit(solution)/shard_map/all_gather | solution.py:48
  16.8 0.0 copy-start.3
  16.8 0.0 copy-start.4
  16.8 0.0 copy-start.5
  16.8 0.0 copy-start.6
  16.8 0.0 copy-start.7
  16.8 0.0 copy-start.8
  16.8 0.9 reshape.31
  17.7 0.0 all-reduce.3.cloned.1.call-update
  17.8 0.0 all-reduce.5.cloned.1.call-start
  17.8 0.0 copy-done.2
  17.8 16.0 %all-gather.2 = f32[4,192,64]{1,2,0:T(8,128)S(1)} all-gather(f32[1,192,64]{1,2,0:T(8,128)S(1)} %bitcast.36), channel_id=1, replica_groups=mesh['groups'=2,'row'=4,'col'=4] {'col'}, dimensions={0}, use_global_device_ids=true | all-gather | bytes 245760 | tf_op jit(solution)/shard_map/all_gather | solution.py:63
  33.9 0.2 copy.31
  34.0 0.9 reshape.44
  34.9 0.0 all-reduce.5.cloned.1.call-update
  34.9 0.0 reduce-scatter.4.cloned.1.call-start
  35.0 0.0 copy-done.3
  35.0 0.0 copy-done.4
  35.0 5.1 %all-gather = s32[4,2,2]{2,1,0:T(2,128)S(1)} all-gather(s32[1,2,2]{2,1,0:T(2,128)S(1)} %add_bitcast_fusion), channel_id=1, replica_groups=mesh['groups'=2,'row'=4,'col'=4] {'row'}, dimensions={0}, use_global_device_ids=true | all-gather | bytes 80 | tf_op jit(solution)/shard_map/all_gather | solution.py:49
  40.1 0.1 copy.34
  40.2 7.8 %psum.21 = s32[8,2]{0,1:T(2,128)S(1)} all-reduce(s32[8,2]{0,1:T(2,128)S(1)} %broadcast_select_fusion.2), channel_id=1, replica_groups=mesh['groups'=2,'row'=4,'col'=4] {'col'}, use_global_device_ids=true, to_apply=%region_0.1 | all-reduce | flops 16 | bytes 128 | tf_op jit(solution)/shard_map/psum | solution.py:12
  47.9 0.1 copy.27
  48.0 0.0 copy-done.5
  48.0 0.0 copy-done.6
  48.1 0.1 select_reduce_fusion
  48.1 0.0 copy-done.7
  48.2 0.1 broadcast_in_dim.32
  48.2 0.2 convert_element_type.38
  48.4 0.0 copy-done.8
  48.4 5.1 %all-gather.1 = bf16[4,1,256]{2,1,0:T(2,128)(2,1)S(1)} all-gather(bf16[1,1,256]{2,1,0:T(2,128)(2,1)S(1)} %reshape.37), channel_id=1, replica_groups=mesh['groups'=2,'row'=4,'col'=4] {'row'}, dimensions={0}, use_global_device_ids=true | all-gather | bytes 2560 | tf_op jit(solution)/shard_map/all_gather | solution.py:50
  53.5 0.2 multiply_convert_fusion
  53.7 0.1 reshape.33
  53.8 2.2 %convolution_convert_fusion = bf16[8,6,128,128]{3,1,2,0:T(8,128)(2,1)} fusion(bf16[8,128,2,128]{3,2,1,0:T(2,128)(2,1)S(1)} %reshape.33, s32[6]{0:T(128)S(1)} %iota_add_fusion, s32[8,2]{1,0:T(8,128)S(1)} %bitcast.38), kind=kOutput, calls=%fused_computation | convolution fusion | flops 3932256 | bytes 2097240 | tf_op jit(solution)/shard_map/rskb,rka->rsab/dot_general | solution.py:21
  56.0 3.4 %all-reduce.3.cloned.1.call-done = bf16[8,128,2,128]{3,2,1,0:T(2,128)(2,1)} async-done(((bf16[8,128,2,128]{3,2,1,0:T(2,128)(2,1)}), bf16[8,128,2,128]{3,2,1,0:T(2,128)(2,1)}) %all-reduce.3.cloned.1.call-update) | async-done | bytes 524304 | tf_op jit(solution)/shard_map/psum | solution.py:12
  59.4 0.0 copy-start.1
  59.4 2.1 %convolution_convert_fusion.1 = bf16[8,6,128,128]{3,1,2,0:T(8,128)(2,1)S(1)} fusion(bf16[8,128,2,128]{3,2,1,0:T(2,128)(2,1)} %all-reduce.3.cloned.1.call-done, s32[6]{0:T(128)S(1)} %iota_add_fusion.1, s32[8,2]{1,0:T(8,128)S(1)} %copy.27), kind=kOutput, calls=%fused_computation.1 | convolution fusion | flops 3932256 | bytes 2097240 | tf_op jit(solution)/shard_map/rskb,rka->rsab/dot_general | solution.py:21
  61.5 0.0 copy-done.1
  61.5 1.5 %fusion = f32[768,768]{1,0:T(8,128)S(1)} fusion(bf16[128,8,6,128]{3,2,1,0:T(8,128)(2,1)S(1)} %bitcast.34, bf16[128,8,6,128]{3,2,1,0:T(8,128)(2,1)S(1)} %bitcast.35), kind=kOutput, calls=%fused_computation.2 | convolution fusion | flops 1207959552 | bytes 5505024 | tf_op jit(solution)/shard_map/dot_general | solution.py:60
  63.0 0.0 copy-start
  63.0 30.5 %all-reduce.5.cloned.1.call-done = f32[768,64]{0,1:T(8,128)} async-done(((f32[768,64]{0,1:T(8,128)}), f32[768,64]{0,1:T(8,128)}) %all-reduce.5.cloned.1.call-update) | async-done | bytes 196624 | tf_op jit(solution)/shard_map/psum | solution.py:12
  93.5 3.7 %fusion.13 = f32[768,64]{1,0:T(8,128)} fusion(f32[768,768]{1,0:T(8,128)S(1)} %fusion, f32[768,64]{0,1:T(8,128)} %all-reduce.5.cloned.1.call-done), kind=kOutput, calls=%fused_computation.27 | convolution fusion | flops 452984832 | bytes 2752512
  97.2 0.0 reduce-scatter.4.cloned.1.call-update
  97.2 21.0 %reduce-scatter.4.cloned.1.call-done = f32[192,64]{1,0:T(8,128)} async-done(((f32[768,64]{1,0:T(8,128)}), f32[192,64]{1,0:T(8,128)}) %reduce-scatter.4.cloned.1.call-update) | async-done | bytes 49168
  118.2 1.6 %copy.38 = f32[192,64]{0,1:T(8,128)} copy(f32[192,64]{1,0:T(8,128)} %reduce-scatter.4.cloned.1.call-done) | data formatting | bytes 98304
  119.8 0.0 copy-done
  (10 shorter events, 0.1 us)
Async XLA Ops:
  7.2 10.7 %copy-start.2 = (f32[192,64]{0,1:T(8,128)S(1)}, f32[192,64]{0,1:T(8,128)}, u32[]{:S(2)}) copy-start(f32[192,64]{0,1:T(8,128)} %param.17) | copy-start | bytes 147460
  7.2 52.2 %all-reduce.3.cloned.1.call-start = ((), (), s32[]{:S(2)}) async-start(), calls=%async_computation.1 | async-start | bytes 1048576 | tf_op jit(solution)/shard_map/psum | solution.py:12
  16.8 18.2 %copy-start.3 = (s32[1,2]{1,0:T(1,128)S(1)}, s32[1,2]{1,0:T(1,128)}, u32[]{:S(2)}) copy-start(s32[1,2]{1,0:T(1,128)} %param.12) | copy-start | bytes 28
  16.8 18.2 %copy-start.4 = (s32[1,2]{1,0:T(1,128)S(1)}, s32[1,2]{1,0:T(1,128)}, u32[]{:S(2)}) copy-start(s32[1,2]{1,0:T(1,128)} %param.11) | copy-start | bytes 28
  16.8 31.3 %copy-start.5 = (f32[16]{0:T(128)S(1)}, f32[16]{0:T(128)}, u32[]{:S(2)}) copy-start(f32[16]{0:T(128)} %param.15) | copy-start | bytes 196
  16.8 31.3 %copy-start.6 = (s32[64]{0:T(128)S(1)}, s32[64]{0:T(128)}, u32[]{:S(2)}) copy-start(s32[64]{0:T(128)} %param.13) | copy-start | bytes 772
  16.8 31.4 %copy-start.7 = (s32[64]{0:T(128)S(1)}, s32[64]{0:T(128)}, u32[]{:S(2)}) copy-start(s32[64]{0:T(128)} %param.14) | copy-start | bytes 772
  16.8 31.6 %copy-start.8 = (bf16[128]{0:T(256)(128)(2,1)S(1)}, bf16[128]{0:T(256)(128)(2,1)}, u32[]{:S(2)}) copy-start(bf16[128]{0:T(256)(128)(2,1)} %param.16) | copy-start | bytes 772
  17.8 75.8 %all-reduce.5.cloned.1.call-start = ((), (), s32[]{:S(2)}) async-start(), calls=%async_computation.2 | async-start | bytes 393216 | tf_op jit(solution)/shard_map/psum | solution.py:12
  34.9 83.3 %reduce-scatter.4.cloned.1.call-start = ((), (), s32[]{:S(2)}) async-start(), calls=%async_computation.3 | async-start | bytes 491520
  59.4 2.1 %copy-start.1 = (bf16[8,6,128,128]{3,1,2,0:T(8,128)(2,1)S(1)}, bf16[8,6,128,128]{3,1,2,0:T(8,128)(2,1)}, u32[]{:S(2)}) copy-start(bf16[8,6,128,128]{3,1,2,0:T(8,128)(2,1)} %convolution_convert_fusion) | copy-start | bytes 4718596
  63.0 56.8 %copy-start = (f32[768,768]{1,0:T(8,128)}, f32[768,768]{1,0:T(8,128)S(1)}, u32[]{:S(2)}) copy-start(f32[768,768]{1,0:T(8,128)S(1)} %fusion) | copy-start | bytes 7077892
Sparse Core Ops, SparseCore 0:
  17.9 41.4 all-reduce.2
  61.7 31.7 all-reduce.4
  97.3 20.8 reduce-scatter.3
where the time goes:
time: 127 us; the launch traced here: 126 us
  waiting for transfers between devices  54.9 us (43%)
  blocking collectives  42.6 us (34%)
  between operations  13.9 us (11%)
  matrix products  9.43 us (7%)
  local copies, waits for them, and re-layouts  4.09 us (3%)
  other arithmetic  1.28 us (1%)
    psum x2, waiting for transfers between devices, from_root(): return lax.psum(block, axis)  33.9 us
    unnamed x4, waiting for transfers between devices  21 us
    all_gather x1, blocking collectives, shards(): frames_rows = lax.all_gather(frames, 'col', axis=0, tiled=True)  16 us
    all_gather x1, blocking collectives, shards(): lax.all_gather(local_rows, 'row', axis=0, tiled=True)  8.65 us
    psum x1, blocking collectives, from_root(): return lax.psum(block, axis)  7.79 us
    all_gather x1, blocking collectives, shards(): lax.all_gather(local_ids, 'row', axis=0, tiled=True)  5.07 us
    all_gather x1, blocking collectives, shards(): lax.all_gather(local_weight, 'row', axis=0, tiled=True)  5.07 us
    dot_general x2, matrix products, expand_blocks(): jnp.einsum('rskb,rka->rsab', shaped, onehot, preferred_element_type=jnp.f...  4.29 us
  transfers between devices with their start and end apart: 3, of which 3 were waited for; matrix products, arithmetic and copies ran while one was open for 6% of the time, Pallas kernels for 0%

commit v1 on v0

--- a/solution.py
+++ b/solution.py
@@ -5,6 +5,12 @@
 
 BS = 128
 AB = 6
+
+
+def tiled_gather(x, axis, dim):
+    count = lax.axis_size(axis)
+    repeats = [count if d == dim else 1 for d in range(x.ndim)]
+    return lax.all_to_all(jnp.tile(x, repeats), axis, split_axis=dim, concat_axis=dim, tiled=True)
 
 
 def from_root(block, axis, owner):
@@ -45,7 +51,7 @@
     local_ids = jnp.concatenate([slope_blocks, prior_blocks], axis=0)
     local_weight = jnp.concatenate([slope_weight, prior_weights], axis=0)
     all_rows, all_ids, all_weight = (
-        lax.all_gather(local_rows, "row", axis=0, tiled=True),
+        tiled_gather(local_rows, "row", 0),
         lax.all_gather(local_ids, "row", axis=0, tiled=True),
         lax.all_gather(local_weight, "row", axis=0, tiled=True),
     )

time: 127 us -> 132 us (1.039)
  blocking collectives: 42.6 us -> 34.6 us
  waiting for transfers between devices: 54.9 us -> 61.9 us
  starting transfers between devices: 0.12 us -> 4.32 us
    all_to_all x0 -> x1, waiting for transfers between devices: none -> 8.77 us  [tiled_gather(): lax.all_to_all(jnp.tile(x, repeats), axis, split_axis=dim, concat_axis=di...]
    all_gather x1 -> x0, blocking collectives: 8.65 us -> none  [shards(): lax.all_gather(local_rows, 'row', axis=0, tiled=True)]
    all_to_all x0 -> x1, starting transfers between devices: none -> 4.24 us  [tiled_gather(): lax.all_to_all(jnp.tile(x, repeats), axis, split_axis=dim, concat_axis=di...]
    psum x2, waiting for transfers between devices: 33.9 us -> 32.1 us  [from_root(): return lax.psum(block, axis)]
  transfers between devices with their start and end apart: 3 -> 4, of which waited for: 3 -> 4; matrix products, arithmetic and copies ran while one was open for 6% -> 7% of each run, Pallas kernels for 0% -> 0%
where the time goes in v1:
time: 132 us
  waiting for transfers between devices  61.9 us (47%)
  blocking collectives  34.6 us (26%)
  between operations  13.9 us (11%)
  matrix products  10.4 us (8%)
  local copies, waits for them, and re-layouts  5.33 us (4%)
  starting transfers between devices  4.32 us (3%)
    psum x2, waiting for transfers between devices, from_root(): return lax.psum(block, axis)  32.1 us
    unnamed x4, waiting for transfers between devices  21 us
    all_gather x1, blocking collectives, shards(): frames_rows = lax.all_gather(frames, 'col', axis=0, tiled=True)  16.7 us
    all_to_all x1, waiting for transfers between devices, tiled_gather(): lax.all_to_all(jnp.tile(x, repeats), axis, split_axis=dim, concat_axis=di...  8.77 us
    psum x1, blocking collectives, from_root(): return lax.psum(block, axis)  7.76 us
    dot_general x2, matrix products, expand_blocks(): jnp.einsum('rskb,rka->rsab', shaped, onehot, preferred_element_type=jnp.f...  5.32 us
    all_gather x1, blocking collectives, shards(): lax.all_gather(local_ids, 'row', axis=0, tiled=True)  5.07 us
    all_gather x1, blocking collectives, shards(): lax.all_gather(local_weight, 'row', axis=0, tiled=True)  5.07 us
  transfers between devices with their start and end apart: 4, of which 4 were waited for; matrix products, arithmetic and copies ran while one was open for 7% of the time, Pallas kernels for 0%

profile of v1, /device:TPU:0, one launch (start us, length us, event | category | flops | bytes accessed | tf_op | source)
XLA Modules:
  0.0 131.5 jit_solution(13831919034107462326)
XLA Ops:
  7.2 0.9 pad_maximum_fusion
  8.0 0.0 copy-start.1
  8.1 0.8 tile.2
  8.9 4.2 %all-to-all-start = ((bf16[4,256,256]{2,1,0:T(8,128)(2,1)}), bf16[4,256,256]{2,1,0:T(8,128)(2,1)S(1)}, u32[]{:S(2)}, u32[]{:S(2)}) async-start(bf16[4,256,256]{2,1,0:T(8,128)(2,1)} %tile.2), calls=%async_computation | async-start | bytes 1048576 | tf_op jit(solution)/shard_map/all_to_all | solution.py:13
  13.1 0.0 all-reduce.3.cloned.1.call-start
  13.1 0.0 copy-start.2
  13.1 0.0 copy-start.3
  13.1 0.0 copy-start.4
  13.2 0.0 copy-start.5
  13.2 0.0 copy-start.6
  13.2 8.8 %all-to-all-done = bf16[4,256,256]{2,1,0:T(8,128)(2,1)S(1)} async-done(((bf16[4,256,256]{2,1,0:T(8,128)(2,1)}), bf16[4,256,256]{2,1,0:T(8,128)(2,1)S(1)}, u32[]{:S(2)}, u32[]{:S(2)}) %all-to-all-start) | async-done | bytes 524320 | tf_op jit(solution)/shard_map/all_to_all | solution.py:13
  22.0 0.0 copy-start.7
  22.0 0.9 reshape.48
  22.9 0.0 all-reduce.3.cloned.1.call-update
  22.9 0.0 all-reduce.5.cloned.1.call-start
  23.0 0.0 copy-done.1
  23.0 16.7 %all-gather.2 = f32[4,192,64]{1,2,0:T(8,128)S(1)} all-gather(f32[1,192,64]{1,2,0:T(8,128)S(1)} %bitcast.34), channel_id=1, replica_groups=mesh['groups'=2,'row'=4,'col'=4] {'col'}, dimensions={0}, use_global_device_ids=true | all-gather | bytes 245760 | tf_op jit(solution)/shard_map/all_gather | solution.py:69
  39.7 0.2 copy.31
  39.9 0.9 reshape.62
  40.7 0.0 all-reduce.5.cloned.1.call-update
  40.8 0.0 reduce-scatter.4.cloned.1.call-start
  40.8 0.0 copy-done.2
  40.8 0.0 copy-done.3
  40.8 5.1 %all-gather = s32[4,2,2]{2,1,0:T(2,128)S(1)} all-gather(s32[1,2,2]{2,1,0:T(2,128)S(1)} %add_bitcast_fusion), channel_id=1, replica_groups=mesh['groups'=2,'row'=4,'col'=4] {'row'}, dimensions={0}, use_global_device_ids=true | all-gather | bytes 80 | tf_op jit(solution)/shard_map/all_gather | solution.py:55
  45.9 0.1 copy.34
  46.0 7.8 %psum.21 = s32[8,2]{0,1:T(2,128)S(1)} all-reduce(s32[8,2]{0,1:T(2,128)S(1)} %broadcast_select_fusion.2), channel_id=1, replica_groups=mesh['groups'=2,'row'=4,'col'=4] {'col'}, use_global_device_ids=true, to_apply=%region_0.1 | all-reduce | flops 16 | bytes 128 | tf_op jit(solution)/shard_map/psum | solution.py:18
  53.8 0.1 copy.27
  53.9 0.0 copy-done.4
  53.9 0.0 copy-done.5
  53.9 0.1 select_reduce_fusion
  54.0 0.0 copy-done.6
  54.0 0.1 broadcast_in_dim.32
  54.0 0.2 convert_element_type.42
  54.2 0.0 copy-done.7
  54.2 5.1 %all-gather.1 = bf16[4,1,256]{2,1,0:T(2,128)(2,1)S(1)} all-gather(bf16[1,1,256]{2,1,0:T(2,128)(2,1)S(1)} %reshape.56), channel_id=1, replica_groups=mesh['groups'=2,'row'=4,'col'=4] {'row'}, dimensions={0}, use_global_device_ids=true | all-gather | bytes 2560 | tf_op jit(solution)/shard_map/all_gather | solution.py:56
  59.3 0.5 reshape.52
  59.8 3.2 %convolution_convert_fusion = bf16[8,6,128,128]{3,1,2,0:T(8,128)(2,1)} fusion(f32[8,128,2,128]{3,2,1,0:T(2,128)S(1)} %reshape.52, f32[8,128]{1,0:T(8,128)S(1)} %bitcast.37, s32[6]{0:T(128)S(1)} %iota_add_fusion, s32[8,2]{1,0:T(8,128)S(1)} %bitcast.36), kind=kOutput, calls=%fused_computation | convolution fusion | flops 4456544 | bytes 2625624 | tf_op jit(solution)/shard_map/rskb,rka->rsab/dot_general | solution.py:27
  63.0 1.6 %all-reduce.3.cloned.1.call-done = bf16[8,128,2,128]{3,2,1,0:T(2,128)(2,1)} async-done(((bf16[8,128,2,128]{3,2,1,0:T(2,128)(2,1)}), bf16[8,128,2,128]{3,2,1,0:T(2,128)(2,1)}) %all-reduce.3.cloned.1.call-update) | async-done | bytes 524304 | tf_op jit(solution)/shard_map/psum | solution.py:18
  64.6 2.1 %convolution_convert_fusion.1 = bf16[8,6,128,128]{3,1,2,0:T(8,128)(2,1)S(1)} fusion(bf16[8,128,2,128]{3,2,1,0:T(2,128)(2,1)} %all-reduce.3.cloned.1.call-done, s32[6]{0:T(128)S(1)} %iota_add_fusion.1, s32[8,2]{1,0:T(8,128)S(1)} %copy.27), kind=kOutput, calls=%fused_computation.1 | convolution fusion | flops 3932256 | bytes 2097240 | tf_op jit(solution)/shard_map/rskb,rka->rsab/dot_general | solution.py:27
  66.7 0.0 copy-done.8
  66.8 1.5 %fusion = f32[768,768]{1,0:T(8,128)S(1)} fusion(bf16[128,8,6,128]{3,2,1,0:T(8,128)(2,1)S(1)} %bitcast.38, bf16[128,8,6,128]{3,2,1,0:T(8,128)(2,1)S(1)} %bitcast.33), kind=kOutput, calls=%fused_computation.2 | convolution fusion | flops 1207959552 | bytes 5505024 | tf_op jit(solution)/shard_map/dot_general | solution.py:66
  68.2 0.0 copy-start
  68.3 30.5 %all-reduce.5.cloned.1.call-done = f32[768,64]{0,1:T(8,128)} async-done(((f32[768,64]{0,1:T(8,128)}), f32[768,64]{0,1:T(8,128)}) %all-reduce.5.cloned.1.call-update) | async-done | bytes 196624 | tf_op jit(solution)/shard_map/psum | solution.py:18
  98.8 3.6 %fusion.14 = f32[768,64]{1,0:T(8,128)} fusion(f32[768,768]{1,0:T(8,128)S(1)} %fusion, f32[768,64]{0,1:T(8,128)} %all-reduce.5.cloned.1.call-done), kind=kOutput, calls=%fused_computation.28 | convolution fusion | flops 452984832 | bytes 2752512
  102.4 0.0 reduce-scatter.4.cloned.1.call-update
  102.4 20.9 %reduce-scatter.4.cloned.1.call-done = f32[192,64]{1,0:T(8,128)} async-done(((f32[768,64]{1,0:T(8,128)}), f32[192,64]{1,0:T(8,128)}) %reduce-scatter.4.cloned.1.call-update) | async-done | bytes 49168
  123.4 1.6 %copy.38 = f32[192,64]{0,1:T(8,128)} copy(f32[192,64]{1,0:T(8,128)} %reduce-scatter.4.cloned.1.call-done) | data formatting | bytes 98304
  125.0 0.0 copy-done
  (11 shorter events, 0.1 us)
Async XLA Ops:
  8.0 14.9 %copy-start.1 = (f32[192,64]{0,1:T(8,128)S(1)}, f32[192,64]{0,1:T(8,128)}, u32[]{:S(2)}) copy-start(f32[192,64]{0,1:T(8,128)} %param.17) | copy-start | bytes 147460
  8.9 13.1 %all-to-all-start = ((bf16[4,256,256]{2,1,0:T(8,128)(2,1)}), bf16[4,256,256]{2,1,0:T(8,128)(2,1)S(1)}, u32[]{:S(2)}, u32[]{:S(2)}) async-start(bf16[4,256,256]{2,1,0:T(8,128)(2,1)} %tile.2), calls=%async_computation | async-start | bytes 1048576 | tf_op jit(solution)/shard_map/all_to_all | solution.py:13
  13.1 51.5 %all-reduce.3.cloned.1.call-start = ((), (), s32[]{:S(2)}) async-start(), calls=%async_computation.2 | async-start | bytes 1048576 | tf_op jit(solution)/shard_map/psum | solution.py:18
  13.1 27.7 %copy-start.2 = (s32[1,2]{1,0:T(1,128)S(1)}, s32[1,2]{1,0:T(1,128)}, u32[]{:S(2)}) copy-start(s32[1,2]{1,0:T(1,128)} %param.12) | copy-start | bytes 28
  13.1 27.7 %copy-start.3 = (s32[1,2]{1,0:T(1,128)S(1)}, s32[1,2]{1,0:T(1,128)}, u32[]{:S(2)}) copy-start(s32[1,2]{1,0:T(1,128)} %param.11) | copy-start | bytes 28
  13.1 40.7 %copy-start.4 = (f32[16]{0:T(128)S(1)}, f32[16]{0:T(128)}, u32[]{:S(2)}) copy-start(f32[16]{0:T(128)} %param.15) | copy-start | bytes 196
  13.2 40.7 %copy-start.5 = (s32[64]{0:T(128)S(1)}, s32[64]{0:T(128)}, u32[]{:S(2)}) copy-start(s32[64]{0:T(128)} %param.13) | copy-start | bytes 772
  13.2 40.8 %copy-start.6 = (s32[64]{0:T(128)S(1)}, s32[64]{0:T(128)}, u32[]{:S(2)}) copy-start(s32[64]{0:T(128)} %param.14) | copy-start | bytes 772
  22.0 32.2 %copy-start.7 = (bf16[128]{0:T(256)(128)(2,1)S(1)}, bf16[128]{0:T(256)(128)(2,1)}, u32[]{:S(2)}) copy-start(bf16[128]{0:T(256)(128)(2,1)} %param.16) | copy-start | bytes 772
  22.9 75.8 %all-reduce.5.cloned.1.call-start = ((), (), s32[]{:S(2)}) async-start(), calls=%async_computation.3 | async-start | bytes 393216 | tf_op jit(solution)/shard_map/psum | solution.py:18
  40.8 82.6 %reduce-scatter.4.cloned.1.call-start = ((), (), s32[]{:S(2)}) async-start(), calls=%async_computation.4 | async-start | bytes 491520
  64.6 2.1 %copy-start.8 = (bf16[8,6,128,128]{3,1,2,0:T(8,128)(2,1)S(1)}, bf16[8,6,128,128]{3,1,2,0:T(8,128)(2,1)}, u32[]{:S(2)}) copy-start(bf16[8,6,128,128]{3,1,2,0:T(8,128)(2,1)} %convolution_convert_fusion) | copy-start | bytes 4718596
  68.2 56.7 %copy-start = (f32[768,768]{1,0:T(8,128)}, f32[768,768]{1,0:T(8,128)S(1)}, u32[]{:S(2)}) copy-start(f32[768,768]{1,0:T(8,128)S(1)} %fusion) | copy-start | bytes 7077892
Sparse Core Ops, SparseCore 0:
  23.1 41.5 all-reduce.2
  66.9 31.7 all-reduce.4
  102.6 20.7 reduce-scatter.3
